TPU v7x, 32 devices: a whole 2x2x4 slice. The times are simulated.
32 devices in a mesh: col: 16 (over z, y, x), row: 2 (over core).
Axes of the slice: x: 2, y: 2, z: 4, core: 2. Of those that a mesh axis runs over, the one named last changes fastest.
Arguments:
- top_rows: float32 [1792, 8192], P(None, ('col', 'row')), may hold values from -0.0625 to 0.0625
- lower_new: float32 [8192, 256], P(('col', 'row')), may hold values from -6 to 6
- block_order: int32 [32, 2], P(('col', 'row')), may hold values from 0 to 1, each once within a row
- corner: float32 [1792, 1792], P('row'), may hold values from -0.125 to 0.125
- target: float32 [1792, 256], P('row'), may hold values from -6 to 6
- coupling: float32 [128, 128], replicated, may hold values from -0.5 to 0.5
- top_right: float32 [14, 128, 128], P('row'), may hold values from -0.5 to 0.5
- top_left: float32 [14, 128, 128], P('row'), may hold values from -0.5 to 0.5
- top_values: float32 [14, 128], P('row'), may hold values from 0.5 to 2
- new_right: float32 [2, 128, 128], replicated, may hold values from -0.5 to 0.5
- new_left: float32 [2, 128, 128], replicated, may hold values from -0.5 to 0.5
- new_values: float32 [2, 128], replicated, may hold values from 0.5 to 2
Outputs:
- solution: float32 [1792, 256], P('row')
Inputs may be any that keep to these rules, and one draw needn't show every extreme that they name: Each row of block_order is an ordering of 0 to 1.
All inputs are finite; a program needn't handle non-finite values.
Results may differ from a plain program's by a relative error of at most 0.0001.
Values sent between devices are 32-bit elements; how exact they have to be, the bound alone decides.
No kernel may reach another device: no remote copies, remote signals or barrier semaphores. Data moves between devices by JAX's collectives and lax.ppermute only.
A program may use at most 64 MiB of HBM per device.

v0:
```python
import jax
import jax.numpy as jnp
from jax import lax
from jax.sharding import PartitionSpec as P

PRECISION = lax.Precision.HIGHEST


def shifted(block, axis, distance):
    devices = range(lax.axis_size(axis))
    route = [(i - distance, i) for i in devices if i - distance in devices]
    return lax.ppermute(block, axis, route)


def solve_block(right_side, left_right, left_left, left_values, col_right, col_left, col_values):
    rotated = jnp.dot(
        jnp.dot(left_left, right_side, precision=PRECISION), col_right, precision=PRECISION
    )
    rotated = rotated / (left_values[:, None] + col_values[None, :])
    return jnp.dot(jnp.dot(left_right, rotated, precision=PRECISION), col_left, precision=PRECISION)


def sweep(
    right_side,
    own_block,
    top_right,
    top_left,
    top_values,
    col_right,
    col_left,
    col_values,
    earlier,
    coupling,
):
    block_size = top_right.shape[1]
    solved = []
    for position in range(top_right.shape[0] - 1, -1, -1):
        offset = position * block_size
        current = right_side[offset : offset + block_size]
        if earlier is not None:
            current = current - jnp.dot(
                earlier[offset : offset + block_size], coupling, precision=PRECISION
            )
        result = solve_block(
            current,
            top_right[position],
            top_left[position],
            top_values[position],
            col_right,
            col_left,
            col_values,
        )
        right_side = right_side - jnp.dot(
            own_block[:, offset : offset + block_size], result, precision=PRECISION
        )
        solved.append(result)
    return jnp.concatenate(solved[::-1], axis=0)


def shards(
    top_rows,
    lower_new,
    block_order,
    corner,
    target,
    coupling,
    top_right,
    top_left,
    top_values,
    new_right,
    new_left,
    new_values,
):
    block_size = coupling.shape[0]
    groups = block_order.shape[1]
    lower_blocks = lower_new.reshape(groups, block_size, 2 * block_size)
    paired = jnp.take(lower_blocks, block_order[0], axis=0).reshape(
        groups * block_size, 2 * block_size
    )
    partial_value = jnp.dot(top_rows, paired, precision=PRECISION)
    half_rows = target.shape[0]
    row_index = lax.axis_index("row")
    own_half = lax.psum_scatter(partial_value, "row", scatter_dimension=0, tiled=True)
    own_rows = lax.psum(own_half, "col")
    right_side = target - own_rows
    total_cols = corner.shape[1]
    row_block = (row_index * half_rows + jnp.arange(half_rows)) // block_size
    col_block = jnp.arange(total_cols) // block_size
    masked = jnp.where(row_block[:, None] < col_block[None, :], corner, jnp.zeros_like(corner))
    own_block = lax.dynamic_slice_in_dim(masked, row_index * half_rows, half_rows, 1)
    next_start = jnp.minimum(row_index + 1, lax.axis_size("row") - 1) * half_rows
    next_block = lax.dynamic_slice_in_dim(masked, next_start, half_rows, 1)
    left_side = right_side[:, :block_size]
    right_part = right_side[:, block_size:]
    first_left = sweep(
        left_side,
        own_block,
        top_right,
        top_left,
        top_values,
        new_right[0],
        new_left[0],
        new_values[0],
        None,
        coupling,
    )
    first_right = sweep(
        right_part,
        own_block,
        top_right,
        top_left,
        top_values,
        new_right[1],
        new_left[1],
        new_values[1],
        first_left,
        coupling,
    )
    below_left, below_right = shifted((first_left, first_right), "row", -1)
    final_left = sweep(
        left_side - jnp.dot(next_block, below_left, precision=PRECISION),
        own_block,
        top_right,
        top_left,
        top_values,
        new_right[0],
        new_left[0],
        new_values[0],
        None,
        coupling,
    )
    final_right = sweep(
        right_part - jnp.dot(next_block, below_right, precision=PRECISION),
        own_block,
        top_right,
        top_left,
        top_values,
        new_right[1],
        new_left[1],
        new_values[1],
        final_left,
        coupling,
    )
    return jnp.concatenate([final_left, final_right], axis=1)


def solution(mesh):
    placed = (
        P(None, ("col", "row")),
        P(("col", "row"), None),
        P(("col", "row"), None),
        P("row", None),
        P("row", None),
        P(),
        P("row", None, None),
        P("row", None, None),
        P("row", None),
        P(),
        P(),
        P(),
    )
    return jax.shard_map(
        shards, mesh=mesh, in_specs=placed, out_specs=P("row", None), check_vma=False
    )
```

profile of v0, /device:TPU:1, one launch (start us, length us, event | category | flops | bytes accessed | tf_op | source)
XLA Modules:
  0.0 218.7 jit_solution(16706956188284991691)
XLA Ops:
  6.6 0.8 fusion.390
  7.4 0.7 compare_and_fusion
  8.2 1.5 gather_fusion
  9.8 4.3 %convolution_bitcast_fusion = f32[1792,256]{0,1:T(8,128)} fusion(f32[256,256]{1,0:T(8,128)S(1)} %bitcast_select_fusion, f32[1792,256]{1,0:T(8,128)S(1)} %copy-done), kind=kOutput, calls=%fused_computation.6 | convolution fusion | flops 1409286144 | bytes 3932160 | tf_op jit(solution)/shard_map/dot_general | solution.py:80
  14.5 1.2 copy.13
  15.8 10.4 %reduce-scatter.2.cloned.1.call-done = f32[896,256]{0,1:T(8,128)} async-done(((f32[1792,256]{0,1:T(8,128)}), f32[896,256]{0,1:T(8,128)}) %reduce-scatter.2.cloned.1.call-update) | async-done | bytes 917520 | tf_op jit(solution)/shard_map/reduce_scatter | solution.py:83
  26.2 6.1 %compare_select_fusion = f32[896,1792]{1,0:T(8,128)} fusion(f32[896,1792]{1,0:T(8,128)} %param.15, s32[1792]{0:T(1024)S(1)} %add_select_fusion, s32[896]{0:T(1024)S(1)} %add_select_fusion.1), kind=kLoop, calls=%fused_computation.1 | loop fusion | flops 3211264 | bytes 12855808 | tf_op jit(solution)/shard_map/jit(_where)/select_n | solution.py:89
  32.4 109.5 %all-reduce.2.cloned.1.call-done = f32[896,256]{0,1:T(8,128)} async-done(((f32[896,256]{0,1:T(8,128)}), f32[896,256]{0,1:T(8,128)}) %all-reduce.2.cloned.1.call-update) | async-done | bytes 917520 | tf_op jit(solution)/shard_map/psum | solution.py:84
  141.9 1.7 sub.135
  144.8 1.7 convolution_subtract_fusion.19
  147.6 1.7 convolution_subtract_fusion.18
  154.0 0.6 convolution_subtract_fusion.15
  157.6 5.0 %collective-permute-start = (f32[896,128]{1,0:T(8,128)S(1)}, f32[896,128]{1,0:T(8,128)S(1)}, u32[]{:S(2)}, u32[]{:S(2)}) collective-permute-start(f32[896,128]{1,0:T(8,128)S(1)} %constant_dynamic-update-slice_fusion), channel_id=1, source_target_pairs={{1,0},{3,2},{5,4},{7,6},{9,8},{11,10},{13,12},{15,14},{17,16},{19,... | collective-permute-start | bytes 1376264 | tf_op jit(solution)/shard_map/ppermute | solution.py:12
  164.1 0.6 convolution_subtract_fusion.9
  166.1 0.6 convolution_subtract_fusion.8
  172.4 0.6 convolution_subtract_fusion.5
  176.6 1.5 collective-permute-start.1
  178.1 3.1 %fusion.4 = f32[896,128]{0,1:T(8,128)S(1)} fusion(f32[896,128]{1,0:T(8,128)S(1)} %collective-permute-done, f32[896,1792]{1,0:T(8,128)S(1)} %copy-done.1, s32[]{:T(128)S(6)} %select_n.55, f32[896,256]{0,1:T(8,128)S(1)} %sub.135), kind=kOutput, calls=%fused_computation.7 | convolution fusion | flops 1233240064 | bytes 4587524 | tf_op jit(solution)/shard_map/dot_general | solution.py:121
  182.4 0.6 convolution_subtract_fusion.14
  193.5 3.4 %fusion.7 = f32[896,128]{0,1:T(8,128)S(1)} fusion(f32[896,128]{1,0:T(8,128)S(1)} %collective-permute-done.1, f32[896,1792]{1,0:T(8,128)S(1)} %copy-done.1, s32[]{:T(128)S(6)} %select_n.55, f32[896,256]{0,1:T(8,128)S(1)} %sub.135), kind=kOutput, calls=%fused_computation.8 | convolution fusion | flops 1233240064 | bytes 4587524 | tf_op jit(solution)/shard_map/dot_general | solution.py:133
  200.1 0.6 convolution_subtract_fusion.3
  202.2 0.6 convolution_subtract_fusion.2
  206.3 0.6 convolution_subtract_fusion
  210.6 1.0 pad_maximum_fusion
  (197 shorter events, 45.1 us)
Async XLA Ops:
  6.5 3.2 %copy-start = (f32[1792,256]{1,0:T(8,128)S(1)}, f32[1792,256]{1,0:T(8,128)}, u32[]{:S(2)}) copy-start(f32[1792,256]{1,0:T(8,128)} %param.12) | copy-start | bytes 5505028
  6.5 8.0 %copy-start.6 = (f32[896,256]{1,0:T(8,128)S(1)}, f32[896,256]{1,0:T(8,128)}, u32[]{:S(2)}) copy-start(f32[896,256]{1,0:T(8,128)} %param.16) | copy-start | bytes 2752516
  6.5 9.2 %copy-start.8 = (f32[2,128]{1,0:T(2,128)S(1)}, f32[2,128]{1,0:T(2,128)}, u32[]{:S(2)}) copy-start(f32[2,128]{1,0:T(2,128)} %param.23) | copy-start | bytes 3076
  6.5 9.2 %copy-start.7 = (f32[7,128]{1,0:T(8,128)S(1)}, f32[7,128]{1,0:T(8,128)}, u32[]{:S(2)}) copy-start(f32[7,128]{1,0:T(8,128)} %param.20) | copy-start | bytes 10756
  6.5 19.6 %reduce-scatter.2.cloned.1.call-start = ((), (), s32[]{:S(2)}) async-start(), calls=%async_computation.1 | async-start | bytes 2752512 | tf_op jit(solution)/shard_map/reduce_scatter | solution.py:83
  14.2 127.7 %all-reduce.2.cloned.1.call-start = ((), (), s32[]{:S(2)}) async-start(), calls=%async_computation.2 | async-start | bytes 1835008 | tf_op jit(solution)/shard_map/psum | solution.py:84
  26.2 117.4 %copy-start.4 = (f32[7,128,128]{2,1,0:T(8,128)S(1)}, f32[7,128,128]{2,1,0:T(8,128)}, u32[]{:S(2)}) copy-start(f32[7,128,128]{2,1,0:T(8,128)} %param.19) | copy-start | bytes 1376260
  26.2 117.6 %copy-start.9 = (f32[2,128,128]{2,1,0:T(8,128)S(1)}, f32[2,128,128]{2,1,0:T(8,128)}, u32[]{:S(2)}) copy-start(f32[2,128,128]{2,1,0:T(8,128)} %param.21) | copy-start | bytes 393220
  26.2 117.9 %copy-start.5 = (f32[7,128,128]{2,1,0:T(8,128)S(1)}, f32[7,128,128]{2,1,0:T(8,128)}, u32[]{:S(2)}) copy-start(f32[7,128,128]{2,1,0:T(8,128)} %param.18) | copy-start | bytes 1376260
  26.2 118.2 %copy-start.2 = (f32[2,128,128]{2,1,0:T(8,128)S(1)}, f32[2,128,128]{2,1,0:T(8,128)}, u32[]{:S(2)}) copy-start(f32[2,128,128]{2,1,0:T(8,128)} %param.22) | copy-start | bytes 393220
  141.9 8.5 %copy-start.1 = (f32[896,1792]{1,0:T(8,128)S(1)}, f32[896,1792]{1,0:T(8,128)}, u32[]{:S(2)}) copy-start(f32[896,1792]{1,0:T(8,128)} %compare_select_fusion) | copy-start | bytes 19267588
  146.4 16.2 %copy-start.3 = (f32[128,128]{1,0:T(8,128)S(1)}, f32[128,128]{1,0:T(8,128)}, u32[]{:S(2)}) copy-start(f32[128,128]{1,0:T(8,128)} %param.17) | copy-start | bytes 196612
  157.6 20.5 %collective-permute-start = (f32[896,128]{1,0:T(8,128)S(1)}, f32[896,128]{1,0:T(8,128)S(1)}, u32[]{:S(2)}, u32[]{:S(2)}) collective-permute-start(f32[896,128]{1,0:T(8,128)S(1)} %constant_dynamic-update-slice_fusion), channel_id=1, source_target_pairs={{1,0},{3,2},{5,4},{7,6},{9,8},{11,10},{13,12},{15,14},{17,16},{19,... | collective-permute-start | bytes 1376264 | tf_op jit(solution)/shard_map/ppermute | solution.py:12
  176.6 16.9 %collective-permute-start.1 = (f32[896,128]{1,0:T(8,128)S(1)}, f32[896,128]{1,0:T(8,128)S(1)}, u32[]{:S(2)}, u32[]{:S(2)}) collective-permute-start(f32[896,128]{1,0:T(8,128)S(1)} %constant_dynamic-update-slice_fusion.14), channel_id=1, source_target_pairs={{1,0},{3,2},{5,4},{7,6},{9,8},{11,10},{13,12},{15,14},{17,16},{19,... | collective-permute-start | bytes 1376264 | tf_op jit(solution)/shard_map/ppermute | solution.py:12
Sparse Core Ops, SparseCore 0:
  14.3 11.8 reduce-scatter.1
  31.4 110.3 all-reduce.1
where the time goes:
time: 222 us; the launch traced here: 219 us
  waiting for transfers between devices  120 us (54%)
  matrix products  63.4 us (29%)
  between operations  15 us (7%)
  other arithmetic  10.5 us (5%)
  starting transfers between devices  6.82 us (3%)
  local copies, waits for them, and re-layouts  3.05 us (1%)
    psum x1, waiting for transfers between devices, shards(): own_rows = lax.psum(own_half, 'col')  109 us
    dot_general x24, matrix products, sweep(): jnp.dot(own_block[:, offset:offset + block_size], result, precision=PRECI...  17.1 us
    reduce_scatter x1, waiting for transfers between devices, shards(): lax.psum_scatter(partial_value, 'row', scatter_dimension=0, tiled=True)  10.4 us
    dot_general x28, matrix products, solve_block(): jnp.dot(jnp.dot(left_left, right_side, precision=PRECISION), col_right, p...  8.09 us
    dot_general x28, matrix products, solve_block(): jnp.dot(left_right, rotated, precision=PRECISION)  7.97 us
    dot_general x28, matrix products, solve_block(): jnp.dot(jnp.dot(left_right, rotated, precision=PRECISION), col_left, prec...  7.97 us
    dot_general x28, matrix products, solve_block(): jnp.dot(left_left, right_side, precision=PRECISION)  7.48 us
    ppermute x2, starting transfers between devices, shifted(): return lax.ppermute(block, axis, route)  6.45 us
  transfers between devices with their start and end apart: 4, of which 2 were waited for; matrix products, arithmetic and copies ran while one was open for 17% of the time, Pallas kernels for 0%

commit v1 on v0

--- a/solution.py
+++ b/solution.py
@@ -81,7 +81,8 @@
     half_rows = target.shape[0]
     row_index = lax.axis_index("row")
     own_half = lax.psum_scatter(partial_value, "row", scatter_dimension=0, tiled=True)
-    own_rows = lax.psum(own_half, "col")
+    parts = lax.all_gather(own_half, "col")
+    own_rows = jnp.sum(parts, axis=0)
     right_side = target - own_rows
     total_cols = corner.shape[1]
     row_block = (row_index * half_rows + jnp.arange(half_rows)) // block_size

time: 222 us -> 297 us (1.34)
  waiting for transfers between devices: 120 us -> 182 us
  local copies, waits for them, and re-layouts: 3.05 us -> 15.1 us
  other arithmetic: 10.5 us -> 17.8 us
  matrix products: 63.4 us -> 59.7 us
    all_gather x0 -> x1, waiting for transfers between devices: none -> 170 us  [shards(): parts = lax.all_gather(own_half, 'col')]
    psum x1 -> x0, waiting for transfers between devices: 109 us -> none  [shards(): own_rows = lax.psum(own_half, 'col')]
    unnamed x41, local copies, waits for them, and re-layouts: 1.42 us -> 13.1 us
    reduce_sum x0 -> x1, other arithmetic: none -> 7.66 us  [shards(): own_rows = jnp.sum(parts, axis=0)]
  transfers between devices with their start and end apart: 4 -> 4, of which waited for: 2 -> 2; matrix products, arithmetic and copies ran while one was open for 17% -> 11% of each run, Pallas kernels for 0% -> 0%
where the time goes in v1:
time: 297 us; the launch traced here: 294 us
  waiting for transfers between devices  182 us (61%)
  matrix products  59.7 us (20%)
  other arithmetic  17.8 us (6%)
  between operations  15.2 us (5%)
  local copies, waits for them, and re-layouts  15.1 us (5%)
  starting transfers between devices  4.48 us (2%)
    all_gather x1, waiting for transfers between devices, shards(): parts = lax.all_gather(own_half, 'col')  170 us
    dot_general x24, matrix products, sweep(): jnp.dot(own_block[:, offset:offset + block_size], result, precision=PRECI...  14.4 us
    unnamed x41, local copies, waits for them, and re-layouts  13.1 us
    reduce_scatter x1, waiting for transfers between devices, shards(): lax.psum_scatter(partial_value, 'row', scatter_dimension=0, tiled=True)  11.8 us
    dot_general x28, matrix products, solve_block(): jnp.dot(jnp.dot(left_right, rotated, precision=PRECISION), col_left, prec...  8.36 us
    dot_general x28, matrix products, solve_block(): jnp.dot(jnp.dot(left_left, right_side, precision=PRECISION), col_right, p...  8.02 us
    dot_general x28, matrix products, solve_block(): jnp.dot(left_left, right_side, precision=PRECISION)  7.95 us
    dot_general x28, matrix products, solve_block(): jnp.dot(left_right, rotated, precision=PRECISION)  7.95 us
  transfers between devices with their start and end apart: 4, of which 2 were waited for; matrix products, arithmetic and copies ran while one was open for 11% of the time, Pallas kernels for 0%

profile of v1, /device:TPU:1, one launch (start us, length us, event | category | flops | bytes accessed | tf_op | source)
XLA Modules:
  0.0 294.0 jit_solution(698916795098454297)
XLA Ops:
  6.5 0.8 fusion.390
  7.3 0.7 compare_and_fusion
  8.1 1.5 gather_fusion
  9.7 4.3 %convolution_bitcast_fusion = f32[1792,256]{0,1:T(8,128)} fusion(f32[256,256]{1,0:T(8,128)S(1)} %bitcast_select_fusion, f32[1792,256]{1,0:T(8,128)S(1)} %copy-done), kind=kOutput, calls=%fused_computation.7 | convolution fusion | flops 1409286144 | bytes 3932160 | tf_op jit(solution)/shard_map/dot_general | solution.py:80
  14.3 11.8 %reduce-scatter.2.cloned.1.call-done = f32[896,256]{0,1:T(8,128)} async-done(((f32[1792,256]{0,1:T(8,128)}), f32[896,256]{0,1:T(8,128)}) %reduce-scatter.2.cloned.1.call-update) | async-done | bytes 917520 | tf_op jit(solution)/shard_map/reduce_scatter | solution.py:83
  26.2 6.0 %compare_select_fusion = f32[896,1792]{1,0:T(8,128)} fusion(f32[896,1792]{1,0:T(8,128)} %param.15, s32[1792]{0:T(1024)S(1)} %add_select_fusion, s32[896]{0:T(1024)S(1)} %add_select_fusion.1), kind=kLoop, calls=%fused_computation.2 | loop fusion | flops 3211264 | bytes 12855808 | tf_op jit(solution)/shard_map/jit(_where)/select_n | solution.py:90
  32.2 169.9 %all-gather.3.cloned.1.call-done = f32[14336,256]{0,1:T(8,128)} async-done(((f32[896,256]{0,1:T(8,128)}), f32[14336,256]{0,1:T(8,128)}) %all-gather.3.cloned.1.call-update) | async-done | bytes 14680080 | tf_op jit(solution)/shard_map/all_gather | solution.py:84
  202.2 12.9 %copy.14 = f32[32,8,16,896]{3,2,1,0:T(8,128)} copy(f32[32,8,16,896]{3,1,2,0:T(8,128)} %bitcast.435) | data formatting | bytes 29360128
  215.1 7.7 %bitcast_reduce_fusion = f32[896,256]{0,1:T(8,128)S(1)} fusion(f32[32,8,16,896]{3,2,1,0:T(8,128)} %copy.14), kind=kLoop, calls=%fused_computation.1 | loop fusion | flops 3440640 | bytes 15597568 | tf_op jit(solution)/shard_map/reduce_sum | solution.py:85
  223.1 1.4 sub.135
  225.8 1.5 convolution_subtract_fusion.19
  228.5 1.5 convolution_subtract_fusion.18
  232.9 0.5 convolution_subtract_fusion.16
  234.3 0.7 fusion.209
  238.5 2.8 collective-permute-start
  254.2 1.5 collective-permute-start.1
  255.7 2.8 fusion.4
  259.6 0.5 convolution_subtract_fusion.14
  266.6 0.5 convolution_subtract_fusion.10
  270.0 3.0 %fusion.7 = f32[896,128]{1,0:T(8,128)S(1)} fusion(f32[896,128]{1,0:T(8,128)S(1)} %collective-permute-done.1, f32[896,1792]{1,0:T(8,128)S(1)} %copy-done.2, s32[]{:T(128)S(6)} %select_n.55, f32[896,256]{1,0:T(8,128)S(1)} %sub.135), kind=kOutput, calls=%fused_computation.9 | convolution fusion | flops 1233240064 | bytes 4587524 | tf_op jit(solution)/shard_map/dot_general | solution.py:134
  274.2 0.5 convolution_subtract_fusion.4
  276.1 0.5 convolution_subtract_fusion.3
  281.8 0.5 convolution_subtract_fusion
  285.8 1.0 pad_maximum_fusion
  (198 shorter events, 43.7 us)
Async XLA Ops:
  6.5 3.2 %copy-start = (f32[1792,256]{1,0:T(8,128)S(1)}, f32[1792,256]{1,0:T(8,128)}, u32[]{:S(2)}) copy-start(f32[1792,256]{1,0:T(8,128)} %param.12) | copy-start | bytes 5505028
  6.5 19.6 %copy-start.8 = (f32[2,128]{1,0:T(2,128)S(1)}, f32[2,128]{1,0:T(2,128)}, u32[]{:S(2)}) copy-start(f32[2,128]{1,0:T(2,128)} %param.23) | copy-start | bytes 3076
  6.5 19.6 %copy-start.7 = (f32[7,128]{1,0:T(8,128)S(1)}, f32[7,128]{1,0:T(8,128)}, u32[]{:S(2)}) copy-start(f32[7,128]{1,0:T(8,128)} %param.20) | copy-start | bytes 10756
  6.5 19.6 %reduce-scatter.2.cloned.1.call-start = ((), (), s32[]{:S(2)}) async-start(), calls=%async_computation.1 | async-start | bytes 2752512 | tf_op jit(solution)/shard_map/reduce_scatter | solution.py:83
  14.1 188.1 %all-gather.3.cloned.1.call-start = ((), (), s32[]{:S(2)}) async-start(), calls=%async_computation.2 | async-start | bytes 15597568 | tf_op jit(solution)/shard_map/all_gather | solution.py:84
  215.1 9.4 %copy-start.5 = (f32[7,128,128]{2,1,0:T(8,128)S(1)}, f32[7,128,128]{2,1,0:T(8,128)}, u32[]{:S(2)}) copy-start(f32[7,128,128]{2,1,0:T(8,128)} %param.19) | copy-start | bytes 1376260
  215.1 9.7 %copy-start.9 = (f32[2,128,128]{2,1,0:T(8,128)S(1)}, f32[2,128,128]{2,1,0:T(8,128)}, u32[]{:S(2)}) copy-start(f32[2,128,128]{2,1,0:T(8,128)} %param.21) | copy-start | bytes 393220
  215.1 10.1 %copy-start.6 = (f32[7,128,128]{2,1,0:T(8,128)S(1)}, f32[7,128,128]{2,1,0:T(8,128)}, u32[]{:S(2)}) copy-start(f32[7,128,128]{2,1,0:T(8,128)} %param.18) | copy-start | bytes 1376260
  215.1 10.3 %copy-start.3 = (f32[2,128,128]{2,1,0:T(8,128)S(1)}, f32[2,128,128]{2,1,0:T(8,128)}, u32[]{:S(2)}) copy-start(f32[2,128,128]{2,1,0:T(8,128)} %param.22) | copy-start | bytes 393220
  223.1 8.1 %copy-start.2 = (f32[896,1792]{1,0:T(8,128)S(1)}, f32[896,1792]{1,0:T(8,128)}, u32[]{:S(2)}) copy-start(f32[896,1792]{1,0:T(8,128)} %compare_select_fusion) | copy-start | bytes 19267588
  227.3 14.0 %copy-start.4 = (f32[128,128]{1,0:T(8,128)S(1)}, f32[128,128]{1,0:T(8,128)}, u32[]{:S(2)}) copy-start(f32[128,128]{1,0:T(8,128)} %param.17) | copy-start | bytes 196612
  238.5 17.2 %collective-permute-start = (f32[896,128]{1,0:T(8,128)S(1)}, f32[896,128]{1,0:T(8,128)S(1)}, u32[]{:S(2)}, u32[]{:S(2)}) collective-permute-start(f32[896,128]{1,0:T(8,128)S(1)} %constant_dynamic-update-slice_fusion), channel_id=1, source_target_pairs={{1,0},{3,2},{5,4},{7,6},{9,8},{11,10},{13,12},{15,14},{17,16},{19,... | collective-permute-start | bytes 1376264 | tf_op jit(solution)/shard_map/ppermute | solution.py:12
  254.2 15.8 %collective-permute-start.1 = (f32[896,128]{1,0:T(8,128)S(1)}, f32[896,128]{1,0:T(8,128)S(1)}, u32[]{:S(2)}, u32[]{:S(2)}) collective-permute-start(f32[896,128]{1,0:T(8,128)S(1)} %constant_dynamic-update-slice_fusion.14), channel_id=1, source_target_pairs={{1,0},{3,2},{5,4},{7,6},{9,8},{11,10},{13,12},{15,14},{17,16},{19,... | collective-permute-start | bytes 1376264 | tf_op jit(solution)/shard_map/ppermute | solution.py:12
  277.7 9.2 %copy-start.1 = (f32[1792,256]{1,0:T(8,128)S(1)}, f32[1792,256]{1,0:T(8,128)}, u32[]{:S(2)}) copy-start(f32[1792,256]{1,0:T(8,128)} %param.12) | copy-start | bytes 5505028
Sparse Core Ops, SparseCore 0:
  14.2 11.8 reduce-scatter.1
  28.8 173.3 all-gather.2
